TPU v7x, 32 devices: a whole 2x2x4 slice. The times are simulated.
32 devices in a mesh: groups: 2 (over y), wide: 8 (over z, x), narrow: 2 (over core).
Axes of the slice: x: 2, y: 2, z: 4, core: 2. Of those that a mesh axis runs over, the one named last changes fastest.
Arguments:
- candidates: bfloat16 [16, 2048, 512], P('groups', ('wide', 'narrow')), parts along dimension 0, may hold values from -6 to 6
- pre_inner: bfloat16 [512, 512], replicated, may hold values from -0.25 to 0.25
- pre_bias: float32 [512], replicated, may hold values from -3 to 3
- pre_outer: bfloat16 [512, 512], replicated, may hold values from -0.25 to 0.25
- user_vector: bfloat16 [16, 512], P('groups'), parts along dimension 0, may hold values from -0.25 to 0.25
- kept_index: int32 [16, 512], P('groups'), parts along dimension 0, may hold values from 0 to 2047, as said below
- slot_request: int32 [16], P('groups'), parts along dimension 0, may hold values from 0 to 7, each once
- history_kv: bfloat16 [16, 2, 512, 512], P(('groups', 'wide'), None, None, 'narrow'), parts along dimension 0, may hold values from -6 to 6
- history_bias: float32 [16, 8, 512], P(('groups', 'wide'), 'narrow'), parts along dimension 0, may hold values from -8 to 404
- history_length: int32 [16], P(('groups', 'wide')), parts along dimension 0, may hold values from 64 to 512, as said below
- query_weight: bfloat16 [512, 512], replicated, may hold values from -0.25 to 0.25
- norm_gain: float32 [512], replicated, may hold values from 0.1 to 1.9
- expert_weight: bfloat16 [8, 512, 256], P('narrow'), may hold values from -0.25 to 0.25
- gate_weight: bfloat16 [512, 64], replicated, may hold values from -0.25 to 0.25
- gate_bias: float32 [8, 8], replicated, may hold values from -4 to 401
- tower_inner: bfloat16 [8, 256, 128], P('narrow'), may hold values from -0.375 to 0.375
- tower_outer: bfloat16 [8, 128], P('narrow'), may hold values from -0.5 to 0.5
Outputs:
- prerank_score: float32 [16, 2048], P('groups', ('wide', 'narrow')), parts along dimension 0
- rank_score: float32 [8, 16, 2048], P(None, 'groups', ('wide', 'narrow')), parts along dimension 1
There are 2 independent parts, one for each index of `groups`. A program takes and returns all parts, laid end to end along the dimension named above; an argument that names none is the same for every part. Nothing has to cross between parts.
Inputs may be any that keep to these rules, and one draw needn't show every extreme that they name: `kept_index`: each row holds 512 distinct candidate numbers; of the candidates of one request in one aligned block of 128 numbers at most 64 are kept, and exactly 64 in some block of every request. `slot_request`: a permutation; slot s belongs to ranking group s. `history_length`: at least one entry equals 512.
All inputs are finite; a program needn't handle non-finite values.
Results may differ from a plain program's by a relative error of at most 0.0085.
Values may be sent and summed in bfloat16 or wider, within the bound.
A program may use at most 64 MiB of HBM per device.

v0:
```python
import jax
import jax.numpy as jnp
from jax import lax
from jax.sharding import PartitionSpec as P


def attend_slot(inputs):
    queries, history, biases, length = inputs
    heads_here = biases.shape[0]
    history_span = history.shape[1]
    head_size = queries.shape[1] // heads_here
    row_count = queries.shape[0]
    history_keys = history[0].reshape(history_span, heads_here, head_size)
    history_values = history[1].reshape(history_span, heads_here, head_size)
    shaped = queries.reshape(row_count, heads_here, head_size)
    scores = jnp.einsum(
        "khd,lhd->hkl", shaped, history_keys, preferred_element_type=jnp.float32
    ) * float(head_size) ** (-0.5)
    scores = scores + biases[:, None, :]
    visible = jnp.arange(history_span, dtype=jnp.int32) < length
    scores = jnp.where(visible[None, None, :], scores, -jnp.inf)
    row_max = jnp.max(scores, axis=2, keepdims=True)
    powers = jnp.exp(scores - row_max)
    weights = (powers / jnp.sum(powers, axis=2, keepdims=True)).astype(jnp.bfloat16)
    attended = jnp.einsum(
        "hkl,lhd->khd", weights, history_values, preferred_element_type=jnp.float32
    )
    return attended.astype(jnp.bfloat16).reshape(row_count, heads_here * head_size)


def on_device(
    candidates,
    pre_inner,
    pre_bias,
    pre_outer,
    user_vector,
    kept_index,
    slot_request,
    history_kv,
    history_bias,
    history_length,
    query_weight,
    norm_gain,
    expert_weight,
    gate_weight,
    gate_bias,
    tower_inner,
    tower_outer,
):
    wide_count = lax.axis_size("wide")
    narrow_count = lax.axis_size("narrow")
    shards = wide_count * narrow_count
    wide_rank = lax.axis_index("wide")
    narrow_rank = lax.axis_index("narrow")
    device_rank = wide_rank * narrow_count + narrow_rank
    requests, shard_len, features = candidates.shape
    kept_count = kept_index.shape[1]
    capacity = 2 * kept_count // shards
    group_size = history_kv.shape[0]
    width = pre_outer.shape[1]
    query_width = query_weight.shape[1]
    head_width = query_width // narrow_count
    tasks_here = tower_inner.shape[0]
    experts_all = gate_bias.shape[1]
    hidden_pre = jax.nn.relu(
        jnp.dot(
            candidates.reshape(requests * shard_len, features),
            pre_inner,
            preferred_element_type=jnp.float32,
        )
        + pre_bias
    ).astype(jnp.bfloat16)
    embedded = (
        jnp.dot(hidden_pre, pre_outer, preferred_element_type=jnp.float32)
        .astype(jnp.bfloat16)
        .reshape(requests, shard_len, width)
    )
    prerank_score = jnp.einsum(
        "rsd,rd->rs", embedded, user_vector, preferred_element_type=jnp.float32
    )
    local_index = kept_index - device_rank * shard_len
    matches = local_index[:, :, None] == jnp.arange(shard_len, dtype=jnp.int32)[None, None, :]
    flags = jnp.any(matches, axis=1)
    places = jnp.cumsum(flags.astype(jnp.int32), axis=1) - 1
    packing = (places[:, None, :] == jnp.arange(capacity, dtype=jnp.int32)[None, :, None]) & flags[
        :, None, :
    ]
    packed = jnp.einsum(
        "rcs,rsd->rcd", packing.astype(jnp.bfloat16), embedded, preferred_element_type=jnp.float32
    ).astype(jnp.bfloat16)
    by_slot = packed[slot_request]
    sending = by_slot
    sending = sending.reshape(requests, 1, capacity, -1)
    arrived = lax.all_to_all(
        lax.all_to_all(sending, "wide", split_axis=0, concat_axis=1, tiled=True),
        "narrow",
        split_axis=3,
        concat_axis=1,
        tiled=True,
    )
    slots_here = wide_rank * group_size + jnp.arange(group_size, dtype=jnp.int32)
    requests_here = slot_request[slots_here]
    kept_here = kept_index[requests_here]
    block_of = kept_here // shard_len
    counts = jnp.sum(
        (block_of[:, :, None] == jnp.arange(shards, dtype=jnp.int32)[None, None, :]).astype(
            jnp.int32
        ),
        axis=1,
    )
    block_ends = jnp.cumsum(counts, axis=1)
    starts = block_ends - counts
    row_ranks = jnp.arange(kept_count, dtype=jnp.int32)
    block_at = jnp.sum(
        (block_ends[:, None, :] <= row_ranks[None, :, None]).astype(jnp.int32), axis=2
    )
    within = row_ranks[None, :] - jnp.take_along_axis(starts, block_at, axis=1)
    anchor = block_at % narrow_count * wide_count + block_at // narrow_count
    flat_rows = anchor * capacity + within
    compact = jnp.take_along_axis(
        arrived.reshape(group_size, shards * capacity, -1), flat_rows[:, :, None], axis=1
    )
    embed_full = lax.all_gather(compact, "narrow", axis=2, tiled=True)
    query_columns = lax.dynamic_slice_in_dim(query_weight, narrow_rank * head_width, head_width, 1)
    queries = (
        jnp.dot(
            embed_full.reshape(group_size * kept_count, width),
            query_columns,
            preferred_element_type=jnp.float32,
        )
        .astype(jnp.bfloat16)
        .reshape(group_size, kept_count, head_width)
    )
    attended = lax.map(attend_slot, (queries, history_kv, history_bias, history_length))
    attend_full = lax.all_gather(attended, "narrow", axis=2, tiled=True)
    rows_all = group_size * kept_count
    mixed_in = embed_full.reshape(rows_all, width).astype(jnp.float32) + attend_full.reshape(
        rows_all, width
    ).astype(jnp.float32)
    normed = (
        mixed_in
        * lax.rsqrt(jnp.mean(mixed_in * mixed_in, axis=1, keepdims=True) + 1e-06)
        * norm_gain
    ).astype(jnp.bfloat16)
    expert_out = jax.nn.relu(
        jnp.einsum("kd,edh->keh", normed, expert_weight, preferred_element_type=jnp.float32)
    ).astype(jnp.bfloat16)
    gate_cols = lax.dynamic_slice_in_dim(
        gate_weight, narrow_rank * tasks_here * experts_all, tasks_here * experts_all, 1
    )
    gate_offsets = lax.dynamic_slice_in_dim(gate_bias, narrow_rank * tasks_here, tasks_here, 0)
    logits = (
        jnp.dot(normed, gate_cols, preferred_element_type=jnp.float32).reshape(
            rows_all, tasks_here, experts_all
        )
        + gate_offsets[None]
    )
    logit_max = jnp.max(logits, axis=2, keepdims=True)
    gate_pow = jnp.exp(logits - logit_max)
    gate_probs = (gate_pow / jnp.sum(gate_pow, axis=2, keepdims=True)).astype(jnp.bfloat16)
    mixture = jnp.einsum(
        "kte,keh->kth",
        gate_probs,
        lax.all_gather(expert_out, "narrow", axis=1, tiled=True),
        preferred_element_type=jnp.float32,
    ).astype(jnp.bfloat16)
    tower_act = jax.nn.relu(
        jnp.einsum("kth,thj->ktj", mixture, tower_inner, preferred_element_type=jnp.float32)
    ).astype(jnp.bfloat16)
    task_logit = jnp.einsum(
        "ktj,tj->kt", tower_act, tower_outer, preferred_element_type=jnp.float32
    )
    task_logit = task_logit.reshape(group_size, kept_count, tasks_here)
    positions = jnp.arange(shards, dtype=jnp.int32)
    shard_at = positions % wide_count * narrow_count + positions // wide_count
    slot_starts = starts[:, shard_at]
    slot_counts = counts[:, shard_at]
    lanes = jnp.arange(capacity, dtype=jnp.int32)
    source_rows = jnp.minimum(
        slot_starts[:, :, None] + lanes[None, None, :], kept_count - 1
    ).reshape(group_size, shards * capacity)
    gathered = jnp.take_along_axis(task_logit, source_rows[:, :, None], axis=1).reshape(
        group_size, shards, capacity, tasks_here
    )
    filled = lanes[None, None, :] < slot_counts[:, :, None]
    returning = jnp.where(filled[:, :, :, None], gathered, 0.0).reshape(
        group_size, narrow_count, wide_count, capacity, tasks_here
    )
    returned = lax.all_to_all(
        lax.all_to_all(returning, "wide", split_axis=2, concat_axis=0, tiled=True),
        "narrow",
        split_axis=1,
        concat_axis=4,
        tiled=True,
    )
    returned = returned.reshape(requests, capacity, -1)
    request_ids = jnp.arange(requests, dtype=jnp.int32)
    slot_of = jnp.sum(
        jnp.where(slot_request[None, :] == request_ids[:, None], request_ids[None, :], 0), axis=1
    )
    by_request = returned[slot_of]
    rank_score = jnp.einsum(
        "rcs,rct->trs", packing.astype(jnp.float32), by_request, precision=lax.Precision.HIGHEST
    )
    return (prerank_score, rank_score)


def solution(mesh):
    return jax.shard_map(
        on_device,
        mesh=mesh,
        in_specs=(
            P("groups", ("wide", "narrow"), None),
            P(),
            P(),
            P(),
            P("groups", None),
            P("groups", None),
            P("groups"),
            P(("groups", "wide"), None, None, "narrow"),
            P(("groups", "wide"), "narrow", None),
            P(("groups", "wide")),
            P(),
            P(),
            P("narrow", None, None),
            P(),
            P(),
            P("narrow", None, None),
            P("narrow", None),
        ),
        out_specs=(P("groups", ("wide", "narrow")), P(None, "groups", ("wide", "narrow"))),
        check_vma=False,
    )
```

profile of v0, /device:TPU:0, one launch (start us, length us, event | category | flops | bytes accessed | tf_op | source)
XLA Modules:
  0.0 108.9 jit_solution(12506975519350942500)
XLA Ops:
  7.2 0.8 broadcast_subtract_fusion
  8.0 0.7 fusion.9
  8.7 0.3 reduce_window_sum.23
  9.0 0.7 compare_select_fusion.15
  9.7 2.5 %convolution_convert_fusion = bf16[1024,512]{1,0:T(8,128)(2,1)S(1)} fusion(bf16[512,512]{1,0:T(8,128)(2,1)} %param.20, bf16[1024,512]{1,0:T(8,128)(2,1)S(1)} %bitcast.140, bf16[512,512]{1,0:T(8,128)(2,1)} %param.18, f32[512]{0:T(512)} %param.19), kind=kOutput, calls=%fused_computation.24 | convolution fusion | flops 1075838976 | bytes 3147776 | tf_op jit(solution)/shard_map/dot_general | solution.py:74
  12.2 0.3 convolution_convert_fusion.1
  12.5 1.4 %gather_fusion.2 = bf16[8,64,512]{2,1,0:T(8,128)(2,1)} fusion(bf16[8,64,512]{2,1,0:T(8,128)(2,1)S(1)} %convolution_convert_fusion.1, s32[1024]{0:T(1024)S(1)} %pad_clamp_fusion.2), kind=kCustom, calls=%fused_computation.2 | custom fusion | bytes 1048608 | tf_op jit(solution)/shard_map/gather | solution.py:91
  13.8 7.3 %all-to-all-start = ((bf16[8,1,64,512]{3,2,1,0:T(8,128)(2,1)}), bf16[8,1,64,512]{3,2,1,0:T(8,128)(2,1)S(1)}, u32[]{:S(2)}, u32[]{:S(2)}) async-start(bf16[8,1,64,512]{3,2,1,0:T(8,128)(2,1)} %bitcast.32), calls=%async_computation | async-start | bytes 1048576 | tf_op jit(solution)/shard_map/all_to_all | solution.py:95
  21.2 0.6 dynamic-slice.6
  23.1 1.1 fusion.74
  25.4 0.7 constant_dynamic-slice_fusion
  26.3 0.2 reduce_window_sum.22
  26.6 0.7 fusion.75
  27.6 4.4 %compare_select_fusion.3 = (s32[512,1]{0,1:T(1,128)S(1)}, s32[512,1]{0,1:T(1,128)S(1)}) fusion(s32[]{:T(128)} %bitcast.23, s32[]{:T(128)} %bitcast.24, s32[]{:T(128)} %bitcast.25, s32[]{:T(128)} %bitcast.26, s32[]{:T(128)} %bitcast.27, s32[]{:T(128)} %bitcast.29, s32[]{:T(128)} %bitcast.28, s32[512,1]{0,1:T(1,128)S(1)} %bitcast.158), kind=kLoop, calls=%fused_computation.90 | loop fusion | flops 7680 | bytes 6172 | tf_op jit(solution)/shard_map/jit(take_along_axis)/gather | solution.py:117
  32.1 5.6 %compare_and_fusion.1 = (pred[512]{0:T(512)(128)(4,1)S(1)}, s32[512]{0:T(512)S(1)}) fusion(s32[512]{0:T(512)S(1)} %convert_reduce_fusion, pred[512]{0:T(512)(128)(4,1)S(1)} %get-tuple-element.58, pred[512]{0:T(512)(128)(4,1)S(1)} %get-tuple-element.56, pred[512]{0:T(512)(128)(4,1)S(1)} %get-tuple-element.57, pred[512]{0:T(512)(128)(4,1)S(1)} %get-tuple-element.55, ...), kind=kLoop, calls=%fused_computation.142 | loop fusion | flops 23040 | bytes 11300 | tf_op jit(solution)/shard_map/jit(take_along_axis)/and | solution.py:120
  37.7 0.8 copy.52
  38.5 0.9 reshape.1055
  39.4 4.2 %all_to_all.60 = bf16[2,2,65536]{2,1,0:T(2,128)(2,1)S(1)} all-to-all(bf16[2,2,65536]{2,1,0:T(2,128)(2,1)S(1)} %reshape.1055), channel_id=1, replica_groups=mesh['groups'=2,'wide'=8,'narrow'=2] {'narrow'}, dimensions={0} | all-to-all | bytes 1048576 | tf_op jit(solution)/shard_map/all_to_all | solution.py:94
  43.6 0.7 reshape.1056
  44.3 0.6 copy.53
  44.9 2.0 %gather_fusion.3 = bf16[512,256]{1,0:T(8,128)(2,1)S(1)} fusion(bf16[1024,256]{1,0:T(8,128)(2,1)S(1)} %bitcast.144, s32[1024]{0:T(1024)S(1)} %pad_clamp_fusion.1), kind=kCustom, calls=%fused_computation.3 | custom fusion | bytes 526336 | tf_op jit(solution)/shard_map/jit(take_along_axis)/gather | solution.py:120
  47.0 2.2 %all_gather.9 = bf16[1,512,512]{2,1,0:T(8,128)(2,1)S(1)} all-gather(bf16[1,512,256]{2,1,0:T(8,128)(2,1)S(1)} %bitcast_select_fusion), channel_id=1, replica_groups=mesh['groups'=2,'wide'=8,'narrow'=2] {'narrow'}, dimensions={2}, use_global_device_ids=true | all-gather | bytes 786432 | tf_op jit(solution)/shard_map/all_gather | solution.py:123
  49.2 1.3 %convolution_convert_fusion.2 = bf16[512,256]{0,1:T(8,128)(2,1)S(1)} fusion(bf16[1,512,512]{2,1,0:T(8,128)(2,1)S(1)} %all_gather.9, bf16[512,512]{1,0:T(8,128)(2,1)} %param.27, s32[]{:T(128)S(6)} %select_n.397), kind=kOutput, calls=%fused_computation.32 | convolution fusion | flops 134348800 | bytes 1048580 | tf_op jit(solution)/shard_map/dot_general | solution.py:126
  50.5 3.6 %fusion.76 = (f32[4,512]{1,0:T(4,128)S(1)}, f32[4,512,512]{1,2,0:T(8,128)}) fusion(f32[4,512]{1,0:T(4,128)S(1)} %bitcast.167, pred[512]{0:T(512)(128)(4,1)S(1)} %iota_compare_fusion.6, bf16[512,4,64]{0,2,1:T(8,128)(2,1)S(1)} %bitcast.154, bf16[512,4,64]{0,2,1:T(8,128)(2,1)S(1)} %bitcast.152), kind=kOutput, calls=%fused_computation.163 | convolution fusion | flops 139461120 | bytes 4735488 | tf_op jit(solution)/shard_map/while/body/eval_jaxpr/sub | solution.py:23
  54.1 2.7 %fusion.17 = bf16[4,512,64]{1,2,0:T(8,128)(2,1)S(1)} fusion(bf16[512,4,64]{0,2,1:T(8,128)(2,1)S(1)} %bitcast.151, f32[4,512,512]{1,2,0:T(8,128)} %get-tuple-element.82, f32[4,512]{1,0:T(4,128)S(1)} %get-tuple-element.81), kind=kOutput, calls=%fused_computation.33 | convolution fusion | flops 136445952 | bytes 4726784 | tf_op jit(solution)/shard_map/while/body/eval_jaxpr/hkl,lhd->khd/dot_general | solution.py:25
  56.9 2.4 %all_gather.10 = bf16[1,512,512]{2,1,0:T(8,128)(2,1)S(1)} all-gather(bf16[1,512,256]{2,1,0:T(8,128)(2,1)S(1)} %copy.57), channel_id=1, replica_groups=mesh['groups'=2,'wide'=8,'narrow'=2] {'narrow'}, dimensions={2}, use_global_device_ids=true | all-gather | bytes 786432 | tf_op jit(solution)/shard_map/all_gather | solution.py:135
  59.3 0.2 multiply_reduce_fusion
  59.5 3.0 %maximum_convert_fusion = bf16[512,4,256]{2,0,1:T(8,128)(2,1)} fusion(bf16[4,512,256]{2,1,0:T(8,128)(2,1)} %param.29, bf16[1,512,512]{2,1,0:T(8,128)(2,1)S(1)} %all_gather.10, bf16[1,512,512]{2,1,0:T(8,128)(2,1)S(1)} %all_gather.9, f32[512]{0:T(512)S(1)} %copy-done.8, f32[512]{0:T(512)S(1)} %add_rsqrt_fusion), kind=kOutput, calls=%fused_computation.14 | convolution fusion | flops 539492352 | bytes 3149824 | tf_op jit(solution)/shard_map/kd,edh->keh/dot_general | solution.py:146
  62.6 0.7 gather_fusion
  63.2 0.7 gather_fusion.1
  64.8 1.0 fusion.51
  65.8 0.4 fusion.77
  66.2 0.3 copy.58
  66.6 8.1 %all-gather.2.cloned.1.call-done = bf16[512,8,256]{2,0,1:T(8,128)(2,1)} async-done(((bf16[512,4,256]{2,0,1:T(8,128)(2,1)}), bf16[512,8,256]{2,0,1:T(8,128)(2,1)}) %all-gather.2.cloned.1.call-update) | async-done | bytes 2097168 | tf_op jit(solution)/shard_map/all_gather | solution.py:164
  74.7 3.1 %fusion.11 = bf16[512,4,256]{2,1,0:T(4,128)(2,1)S(1)} fusion(bf16[512,4,8]{2,1,0:T(4,128)(2,1)S(1)} %copy.58, bf16[512,8,256]{2,0,1:T(8,128)(2,1)} %all-gather.2.cloned.1.call-done), kind=kOutput, calls=%fused_computation.23 | convolution fusion | flops 8912896 | bytes 3178496 | tf_op jit(solution)/shard_map/kte,keh->kth/dot_general | solution.py:161
  77.8 0.6 fusion.16
  78.6 2.8 %gather_fusion.4 = f32[1024,4]{1,0:T(8,128)S(1)} fusion(f32[512,4]{1,0:T(8,128)S(1)} %bitcast.143, s32[1024]{0:T(1024)S(1)} %broadcast_clamp_fusion), kind=kCustom, calls=%fused_computation.4 | custom fusion | bytes 36864 | tf_op jit(solution)/shard_map/jit(take_along_axis)/gather | solution.py:182
  81.4 0.2 copy.61
  81.7 0.7 reshape.1057
  82.4 5.8 %all-to-all-start.2 = ((f32[8,1,512]{2,1,0:T(1,128)}), f32[8,1,512]{2,1,0:T(1,128)S(1)}, u32[]{:S(2)}, u32[]{:S(2)}) async-start(f32[8,1,512]{2,1,0:T(1,128)} %reshape.1057), calls=%async_computation.2 | async-start | bytes 32768 | tf_op jit(solution)/shard_map/all_to_all | solution.py:190
  88.1 6.6 %all-to-all-done.2 = f32[8,1,512]{2,1,0:T(1,128)S(1)} async-done(((f32[8,1,512]{2,1,0:T(1,128)}), f32[8,1,512]{2,1,0:T(1,128)S(1)}, u32[]{:S(2)}, u32[]{:S(2)}) %all-to-all-start.2) | async-done | bytes 16416 | tf_op jit(solution)/shard_map/all_to_all | solution.py:190
  94.7 0.5 broadcast.1393
  95.2 0.7 reduce.24
  96.1 3.7 %all_to_all.61 = f32[2,1,2048]{2,1,0:T(1,128)S(1)} all-to-all(f32[2,1,2048]{2,1,0:T(1,128)S(1)} %reshape.1059), channel_id=1, replica_groups=mesh['groups'=2,'wide'=8,'narrow'=2] {'narrow'}, dimensions={0} | all-to-all | bytes 32768 | tf_op jit(solution)/shard_map/all_to_all | solution.py:189
  99.8 0.7 reduce.25
  100.6 0.6 gather_fusion.5
  101.2 0.2 convolution_bitcast_fusion
  101.4 0.6 copy.64
  (67 shorter events, 2.4 us)
Async XLA Ops:
  7.2 2.5 %copy-start = (bf16[8,128,512]{2,1,0:T(8,128)(2,1)S(1)}, bf16[8,128,512]{2,1,0:T(8,128)(2,1)}, u32[]{:S(2)}) copy-start(bf16[8,128,512]{2,1,0:T(8,128)(2,1)} %param.17) | copy-start | bytes 3145732
  12.1 12.0 %copy-start.1 = (bf16[1024,512]{1,0:T(8,128)(2,1)}, bf16[1024,512]{1,0:T(8,128)(2,1)S(1)}, u32[]{:S(2)}) copy-start(bf16[1024,512]{1,0:T(8,128)(2,1)S(1)} %convolution_convert_fusion) | copy-start | bytes 3145732
  12.1 9.0 %copy-start.10 = (s32[8]{0:T(128)S(1)}, s32[8]{0:T(128)}, u32[]{:S(2)}) copy-start(s32[8]{0:T(128)} %param.23) | copy-start | bytes 100
  13.8 23.9 %all-to-all-start = ((bf16[8,1,64,512]{3,2,1,0:T(8,128)(2,1)}), bf16[8,1,64,512]{3,2,1,0:T(8,128)(2,1)S(1)}, u32[]{:S(2)}, u32[]{:S(2)}) async-start(bf16[8,1,64,512]{3,2,1,0:T(8,128)(2,1)} %bitcast.32), calls=%async_computation | async-start | bytes 1048576 | tf_op jit(solution)/shard_map/all_to_all | solution.py:95
  21.1 53.6 %all-gather.2.cloned.1.call-start = ((), (), s32[]{:S(2)}) async-start(), calls=%async_computation.4 | async-start | bytes 3145728 | tf_op jit(solution)/shard_map/all_gather | solution.py:164
  44.9 5.6 %copy-start.7 = (f32[1,4,512]{2,1,0:T(4,128)S(1)}, f32[1,4,512]{2,1,0:T(4,128)}, u32[]{:S(2)}) copy-start(f32[1,4,512]{2,1,0:T(4,128)} %param.25) | copy-start | bytes 24580
  56.7 2.8 %copy-start.8 = (f32[512]{0:T(512)S(1)}, f32[512]{0:T(512)}, u32[]{:S(2)}) copy-start(f32[512]{0:T(512)} %param.28) | copy-start | bytes 6148
  62.5 2.0 %copy-start.4 = (f32[8,8]{1,0:T(8,128)S(1)}, f32[8,8]{1,0:T(8,128)}, u32[]{:S(2)}) copy-start(f32[8,8]{1,0:T(8,128)} %param.31) | copy-start | bytes 772
  62.5 2.2 %copy-start.2 = (bf16[1024,512]{1,0:T(8,128)(2,1)S(1)}, bf16[1024,512]{1,0:T(8,128)(2,1)}, u32[]{:S(2)}) copy-start(bf16[1024,512]{1,0:T(8,128)(2,1)} %copy-done.1) | copy-start | bytes 3145732
  62.5 2.3 %copy-start.3 = (bf16[8,512]{1,0:T(8,128)(2,1)S(1)}, bf16[8,512]{1,0:T(8,128)(2,1)}, u32[]{:S(2)}) copy-start(bf16[8,512]{1,0:T(8,128)(2,1)} %param.21) | copy-start | bytes 24580
  62.5 3.2 %copy-start.6 = (bf16[512,64]{0,1:T(8,128)(2,1)S(1)}, bf16[512,64]{0,1:T(8,128)(2,1)}, u32[]{:S(2)}) copy-start(bf16[512,64]{0,1:T(8,128)(2,1)} %param.30) | copy-start | bytes 196612
  66.2 11.6 %copy-start.5 = (bf16[4,256,128]{2,1,0:T(8,128)(2,1)S(1)}, bf16[4,256,128]{2,1,0:T(8,128)(2,1)}, u32[]{:S(2)}) copy-start(bf16[4,256,128]{2,1,0:T(8,128)(2,1)} %param.32) | copy-start | bytes 786436
  66.2 11.6 %copy-start.9 = (bf16[4,128]{1,0:T(4,128)(2,1)S(1)}, bf16[4,128]{1,0:T(4,128)(2,1)}, u32[]{:S(2)}) copy-start(bf16[4,128]{1,0:T(4,128)(2,1)} %param.33) | copy-start | bytes 3076
  82.4 12.4 %all-to-all-start.2 = ((f32[8,1,512]{2,1,0:T(1,128)}), f32[8,1,512]{2,1,0:T(1,128)S(1)}, u32[]{:S(2)}, u32[]{:S(2)}) async-start(f32[8,1,512]{2,1,0:T(1,128)} %reshape.1057), calls=%async_computation.2 | async-start | bytes 32768 | tf_op jit(solution)/shard_map/all_to_all | solution.py:190
Sparse Core Ops, SparseCore 0:
  62.7 11.9 all-gather.1
where the time goes:
time: 110 us; the launch traced here: 109 us
  matrix products  18.6 us (17%)
  local copies, waits for them, and re-layouts  17.9 us (16%)
  between operations  17.1 us (16%)
  other arithmetic  15.1 us (14%)
  waiting for transfers between devices  14.7 us (13%)
  starting transfers between devices  13.1 us (12%)
  blocking collectives  12.4 us (11%)
    all_gather x1, waiting for transfers between devices, on_device(): lax.all_gather(expert_out, 'narrow', axis=1, tiled=True)  8.12 us
    all_to_all x1, starting transfers between devices, on_device(): lax.all_to_all(sending, 'wide', split_axis=0, concat_axis=1, tiled=True)  7.28 us
    all_to_all x1, waiting for transfers between devices, on_device(): lax.all_to_all(returning, 'wide', split_axis=2, concat_axis=0, tiled=True)  6.57 us
    all_to_all x1, starting transfers between devices, on_device(): lax.all_to_all(returning, 'wide', split_axis=2, concat_axis=0, tiled=True)  5.78 us
    and x1, other arithmetic, on_device(): jnp.take_along_axis(arrived.reshape(group_size, shards * capacity, -1), f...  5.6 us
    gather x2, other arithmetic, on_device(): within = row_ranks[None, :] - jnp.take_along_axis(starts, block_at, axis=1)  4.48 us
    all_to_all x1, blocking collectives, on_device(): lax.all_to_all(lax.all_to_all(sending, 'wide', split_axis=0, concat_axis=...  4.15 us
    all_to_all x1, blocking collectives, on_device(): lax.all_to_all(lax.all_to_all(returning, 'wide', split_axis=2, concat_axi...  3.72 us
  transfers between devices with their start and end apart: 3, of which 2 were waited for; matrix products, arithmetic and copies ran while one was open for 16% of the time, Pallas kernels for 0%

commit v1 on v0

v1 whole, which is shorter than its diff:
```python
import functools

import jax
import jax.numpy as jnp
from jax import lax
from jax.experimental import pallas as pl
from jax.experimental.pallas import tpu as pltpu
from jax.sharding import PartitionSpec as P

F32 = jnp.float32
BF16 = jnp.bfloat16
MESH = pl.DeviceIdType.MESH


def quotient(x, n):
    if n & (n - 1) == 0:
        return lax.shift_right_logical(x, jnp.full_like(x, n.bit_length() - 1))
    return lax.div(x, jnp.full_like(x, n))


def iota(shape, dim):
    return lax.broadcasted_iota(jnp.int32, shape, dim)


def loop(count, body):
    if count <= 16:
        for i in range(count):
            body(i)
    else:
        lax.fori_loop(0, count, lambda i, _: (body(i), 0)[1], 0)


def dot(a, b, dims=((1,), (0,))):
    return lax.dot_general(a, b, (dims, ((), ())), preferred_element_type=F32)


def cascade(
    wide,
    narrow,
    block,
    slot_request,
    slot_of,
    length,
    kept,
    user,
    pre_bias,
    norm_gain,
    gate_bias,
    cand_hbm,
    inner_hbm,
    outer_hbm,
    query_hbm,
    kv_hbm,
    bias_hbm,
    expert_hbm,
    gate_hbm,
    tower_hbm,
    last_hbm,
    score_out,
    rank_out,
    cand,
    inner,
    outer,
    query,
    kv,
    bias,
    expert,
    gate,
    tower,
    last,
    outgoing,
    arrived,
    compaction,
    expert_out,
    mixed,
    going,
    returned,
    local_sem,
    row_send,
    row_recv,
    swap_send,
    swap_recv,
    back_send,
    back_recv,
):
    w = lax.axis_index("wide")
    n = lax.axis_index("narrow")
    shards = wide * narrow
    me = w * narrow + n
    requests, shard_len, _ = cand.shape
    kept_count = kept.shape[1]
    rows = kept_count // narrow
    tasks = gate_bias.shape[0]
    experts = gate_bias.shape[1]
    heads_here = bias.shape[1]

    barrier = pltpu.get_barrier_semaphore()

    def greet(k):
        d = lax.rem(me + k + 1, shards)
        pl.semaphore_signal(
            barrier,
            inc=1,
            device_id={"wide": d // narrow, "narrow": lax.rem(d, narrow)},
            device_id_type=MESH,
        )

    loop(shards - 1, greet)

    plain = [
        pltpu.make_async_copy(src, dst, local_sem.at[k])
        for k, (src, dst) in enumerate(
            (
                (cand_hbm, cand),
                (inner_hbm, inner),
                (outer_hbm, outer),
                (query_hbm, query),
                (gate_hbm, gate),
            )
        )
    ]
    shared = ((kv_hbm.at[0], kv), (bias_hbm.at[0], bias), (expert_hbm, expert), (tower_hbm, tower), (last_hbm, last))
    own = [
        pltpu.make_async_copy(src, dst.at[n], local_sem.at[len(plain) + k])
        for k, (src, dst) in enumerate(shared)
    ]
    for copy in plain + own:
        copy.start()

    base = me * shard_len
    local = base + iota((shard_len, 1), 0)

    def pack(req, emb):
        row = kept[pl.ds(req, 1), :]
        below = jnp.sum((row < local).astype(F32), axis=1, keepdims=True).astype(jnp.int32)
        here = jnp.sum((row == local).astype(F32), axis=1, keepdims=True) > 0.5
        start = below[0:1]
        level = quotient(below, narrow)
        core = below - level * narrow
        place = level - quotient(start + (narrow - 1) - core, narrow)
        place = jnp.where(here, core * block + place, -1)
        packing = (place == iota((1, narrow * block), 1)).astype(F32).astype(BF16)
        return dot(packing, emb, ((0,), (0,))).astype(BF16)

    def score(req, emb):
        every = dot(user[...], emb, ((1,), (1,)))
        score_out[...] += jnp.where(iota((requests, 1), 0) == req, every, 0.0)

    score_out[...] = jnp.zeros_like(score_out)
    for copy in plain[:3]:
        copy.wait()

    def row_copy(i, g, p):
        return pltpu.make_async_remote_copy(
            src_ref=outgoing.at[i, p],
            dst_ref=arrived.at[me],
            send_sem=row_send.at[i, p],
            recv_sem=row_recv.at[me],
            device_id={"wide": g, "narrow": p},
            device_id_type=MESH,
        )

    def embed(x):
        hidden = jnp.maximum(dot(x, inner[...]) + pre_bias[...], 0.0).astype(BF16)
        return dot(hidden, outer[...]).astype(BF16)

    def serve(i, g, req, emb):
        packed = pack(req, emb)
        for p in range(narrow):
            outgoing[i, p] = packed[p * block : (p + 1) * block]

    def send(i, g):
        for p in range(narrow):
            row_copy(i, g, p).start()

    def swaps(k):
        other = lax.rem(n + k, narrow)
        return [
            pltpu.make_async_remote_copy(
                src_ref=src,
                dst_ref=dst.at[n],
                send_sem=swap_send.at[k, a],
                recv_sem=swap_recv.at[k, a],
                device_id={"narrow": other},
                device_id_type=MESH,
            )
            for a, (src, dst) in enumerate(shared)
        ]

    pair = 2 if shard_len % 16 == 0 and wide % 2 == 0 and wide <= 16 else 1
    if pair == 2:
        order = sorted(range(wide), key=lambda d: (abs(2 * d - wide), d))
        order = [d for d in order if d] + [0]
        for first in range(0, wide, 2):
            slots = [lax.rem(w + order[first + a], wide) for a in range(2)]
            reqs = [slot_request[g] for g in slots]
            both = embed(jnp.concatenate([cand[r] for r in reqs], axis=0))
            for a in range(2):
                emb = both[a * shard_len : (a + 1) * shard_len]
                serve(first + a, slots[a], reqs[a], emb)
                score(reqs[a], emb)
            if first == 0:
                pl.semaphore_wait(barrier, shards - 1)
            for a in range(2):
                if order[first + a]:
                    send(first + a, slots[a])
            if first == 2 or wide == 2:
                for k in range(1, narrow):
                    for copy in swaps(k):
                        copy.start()
    else:
        pl.semaphore_wait(barrier, shards - 1)
        for k in range(1, narrow):
            for copy in swaps(k):
                copy.start()

        def one(i):
            g = lax.rem(w + i + 1, wide)
            req = slot_request[g]
            emb = embed(cand[req])
            serve(i, g, req, emb)
            score(req, emb)

        def one_sent(i):
            one(i)
            send(i, lax.rem(w + i + 1, wide))

        loop(wide - 1, one_sent)
        one(wide - 1)
    for k in range(1, narrow):
        row_copy(wide - 1, w, lax.rem(n + k, narrow)).start()
    arrived[me] = outgoing[wide - 1, n]

    request = slot_request[w]
    row = kept[pl.ds(request, 1), :].astype(F32)
    column = jnp.transpose(jnp.broadcast_to(row, (128, kept_count)))[:, 0:1]
    rank = jnp.sum((column < row).astype(F32), axis=0, keepdims=True)
    line = iota((rows, 1), 0)
    wanted = (line * narrow + n).astype(F32)
    chosen = jnp.sum(jnp.where(rank == wanted, row, 0.0), axis=1, keepdims=True)
    chosen = chosen.astype(jnp.int32)
    shard = quotient(chosen, shard_len)
    start = jnp.sum(
        (row < (shard * shard_len).astype(F32)).astype(F32), axis=1, keepdims=True
    ).astype(jnp.int32)
    spot = shard * block + line - quotient(start + (narrow - 1) - n, narrow)
    compaction[...] = (spot == iota((1, shards * block), 1)).astype(F32).astype(BF16)

    for copy in plain[3:] + own:
        copy.wait()
    for k in range(1, narrow):
        for copy in swaps(k):
            copy.wait_recv()

    def rows_in(k):
        d = lax.rem(me + k + 1, shards)
        pltpu.make_async_remote_copy(
            src_ref=outgoing.at[0, 0],
            dst_ref=arrived.at[d],
            send_sem=row_send.at[0, 0],
            recv_sem=row_recv.at[d],
            device_id={"wide": d // narrow, "narrow": lax.rem(d, narrow)},
            device_id_type=MESH,
        ).wait_recv()

    loop(shards - 1, rows_in)
    width = arrived.shape[2]
    embedded = dot(compaction[...], arrived[...].reshape(shards * block, width)).astype(BF16)
    heads = heads_here * narrow
    size = query.shape[1] // heads
    queries = dot(embedded, query[...]).astype(BF16).astype(F32) * float(size) ** (-0.5)
    span = kv.shape[2]
    seen = iota((1, span), 1) < length[0]
    side = 128 // size if 128 % size == 0 and heads_here % (128 // size) == 0 else 1
    strip = side * size
    lane = iota((1, strip), 1)
    pieces = []
    for first in range(0, heads, side):
        c, h = first // heads_here, first % heads_here
        keys = kv[c, 0, :, h * size : h * size + strip]
        values = kv[c, 1, :, h * size : h * size + strip]
        q = queries[:, first * size : first * size + strip]
        out = None
        for a in range(side):
            mine = (lane >= a * size) & (lane < (a + 1) * size)
            s = dot(jnp.where(mine, q, 0.0).astype(BF16), keys, ((1,), (1,)))
            s = s + jnp.where(seen, bias[c, h + a : h + a + 1, :], -jnp.inf)
            top = jnp.max(s, axis=1, keepdims=True)
            powers = jnp.exp(s - top)
            total = jnp.sum(powers, axis=1, keepdims=True)
            part = dot(powers.astype(BF16), values) / total
            out = part if out is None else jnp.where(mine, part, out)
        pieces.append(out.astype(BF16))
    attended = jnp.concatenate(pieces, axis=1)
    u = embedded.astype(F32) + attended.astype(F32)
    normed = (
        u * lax.rsqrt(jnp.mean(u * u, axis=1, keepdims=True) + 1e-06) * norm_gain[...]
    ).astype(BF16)

    logits = dot(gate[...], normed, ((0,), (1,)))
    diagonal = iota((experts, experts), 0) == iota((experts, experts), 1)
    probs = []
    for t in range(tasks):
        offset = jnp.sum(
            jnp.where(diagonal, gate_bias[t : t + 1, :], 0.0), axis=1, keepdims=True
        )
        x = logits[t * experts : (t + 1) * experts] + offset
        x = jnp.exp(x - jnp.max(x, axis=0, keepdims=True))
        probs.append(x / jnp.sum(x, axis=0, keepdims=True))
    fill = -(tasks * experts) % 128
    if fill:
        probs.append(jnp.zeros((fill, rows), F32))
    probs = jnp.transpose(jnp.concatenate(probs, axis=0).astype(BF16).astype(F32))

    experts_here = expert.shape[1]
    for e in range(experts):
        out = dot(normed, expert[e // experts_here, e % experts_here])
        expert_out[e] = jnp.maximum(out, 0.0).astype(BF16).astype(F32)
    step = 64 if rows % 64 == 0 else rows
    for t in range(tasks):
        for r in range(0, rows, step):
            acc = None
            for e in range(experts):
                k = t * experts + e
                term = probs[r : r + step, k : k + 1] * expert_out[e, r : r + step]
                acc = term if acc is None else acc + term
            mixed[t, r : r + step] = acc.astype(BF16)
    tasks_here = tower.shape[1]
    final = jnp.zeros((tasks, rows), F32)
    for t in range(tasks):
        c, h = t // tasks_here, t % tasks_here
        act = jnp.maximum(dot(mixed[t], tower[c, h]), 0.0).astype(BF16)
        weights = last[c, h : h + 1, :].astype(F32)
        weights = jnp.where(iota((tasks, 1), 0) == t, weights, 0.0).astype(BF16)
        final = final + dot(weights, act, ((1,), (1,)))

    high = final.astype(BF16)
    rest = final - high.astype(F32)
    middle = rest.astype(BF16)
    low = (rest - middle.astype(F32)).astype(BF16)
    lanes = going.shape[2]

    def back_copy(d):
        return pltpu.make_async_remote_copy(
            src_ref=going.at[d],
            dst_ref=returned.at[me],
            send_sem=back_send.at[d],
            recv_sem=back_recv.at[me],
            device_id={"wide": d // narrow, "narrow": lax.rem(d, narrow)},
            device_id_type=MESH,
        )

    def scatter(k):
        d = lax.rem(me + k + 1, shards)
        spread = (chosen == d * shard_len + iota((1, lanes), 1)).astype(F32).astype(BF16)
        going[d] = dot(high, spread) + dot(middle, spread) + dot(low, spread)

    def scatter_send(k):
        scatter(k)
        back_copy(lax.rem(me + k + 1, shards)).start()

    loop(shards - 1, scatter_send)
    scatter(shards - 1)
    returned[me] = going[me]

    def back_in(k):
        d = lax.rem(me + k + 1, shards)
        pltpu.make_async_remote_copy(
            src_ref=going.at[0],
            dst_ref=returned.at[d],
            send_sem=back_send.at[0],
            recv_sem=back_recv.at[d],
            device_id={"wide": d // narrow, "narrow": lax.rem(d, narrow)},
            device_id_type=MESH,
        ).wait_recv()

    loop(shards - 1, back_in)

    def deliver(r):
        total = returned[slot_of[r] * narrow]
        for p in range(1, narrow):
            total = total + returned[slot_of[r] * narrow + p]
        rank_out[r] = total[:, :shard_len]

    loop(requests, deliver)

    def rows_out(i):
        for p in range(narrow):
            row_copy(i, w, p).wait_send()

    loop(wide - 1, rows_out)
    for k in range(1, narrow):
        row_copy(wide - 1, w, lax.rem(n + k, narrow)).wait_send()
        for copy in swaps(k):
            copy.wait_send()
    loop(shards - 1, lambda k: back_copy(lax.rem(me + k + 1, shards)).wait_send())


def on_device(
    candidates,
    pre_inner,
    pre_bias,
    pre_outer,
    user_vector,
    kept_index,
    slot_request,
    history_kv,
    history_bias,
    history_length,
    query_weight,
    norm_gain,
    expert_weight,
    gate_weight,
    gate_bias,
    tower_inner,
    tower_outer,
):
    wide = lax.axis_size("wide")
    narrow = lax.axis_size("narrow")
    shards = wide * narrow
    requests, shard_len, features = candidates.shape
    kept_count = kept_index.shape[1]
    assert history_kv.shape[0] == 1 and requests == wide and kept_count % narrow == 0
    capacity = 2 * kept_count // shards
    block = -(-capacity // narrow)
    block = -(-block // 16) * 16
    rows = kept_count // narrow
    width = pre_outer.shape[1]
    tasks, experts = gate_bias.shape
    hidden = expert_weight.shape[2]
    lanes = max(shard_len, 128)
    ids = jnp.arange(requests, dtype=jnp.int32)
    slot_of = jnp.sum(jnp.where(slot_request[None, :] == ids[:, None], ids[None, :], 0), axis=1)
    smem = pl.BlockSpec(memory_space=pltpu.SMEM)
    vmem = pl.BlockSpec(memory_space=pltpu.VMEM)
    hbm = pl.BlockSpec(memory_space=pl.ANY)

    def whole(x):
        return pltpu.VMEM(x.shape, x.dtype)

    def both(x):
        return pltpu.VMEM((narrow, *x.shape), x.dtype)

    score, rank = pl.pallas_call(
        functools.partial(cascade, wide, narrow, block),
        out_shape=(
            jax.ShapeDtypeStruct((requests, shard_len), F32),
            jax.ShapeDtypeStruct((requests, tasks, shard_len), F32),
        ),
        in_specs=[smem] * 3 + [vmem] * 5 + [hbm] * 10,
        out_specs=(vmem, vmem),
        scratch_shapes=[
            whole(candidates),
            whole(pre_inner),
            whole(pre_outer),
            whole(query_weight),
            pltpu.VMEM((narrow, *history_kv.shape[1:]), BF16),
            pltpu.VMEM((narrow, *history_bias.shape[1:]), F32),
            both(expert_weight),
            whole(gate_weight),
            both(tower_inner),
            both(tower_outer),
            pltpu.VMEM((wide, narrow, block, width), BF16),
            pltpu.VMEM((shards, block, width), BF16),
            pltpu.VMEM((rows, shards * block), BF16),
            pltpu.VMEM((experts, rows, hidden), F32),
            pltpu.VMEM((tasks, rows, hidden), BF16),
            pltpu.VMEM((shards, tasks, lanes), F32),
            pltpu.VMEM((shards, tasks, lanes), F32),
            pltpu.SemaphoreType.DMA((10,)),
            pltpu.SemaphoreType.DMA((wide, narrow)),
            pltpu.SemaphoreType.DMA((shards,)),
            pltpu.SemaphoreType.DMA((narrow, 5)),
            pltpu.SemaphoreType.DMA((narrow, 5)),
            pltpu.SemaphoreType.DMA((shards,)),
            pltpu.SemaphoreType.DMA((shards,)),
        ],
        compiler_params=pltpu.CompilerParams(
            collective_id=0, has_side_effects=True, vmem_limit_bytes=56 * 1024 * 1024
        ),
    )(
        slot_request,
        slot_of,
        history_length,
        kept_index,
        user_vector,
        pre_bias.reshape(1, -1),
        norm_gain.reshape(1, -1),
        gate_bias,
        candidates,
        pre_inner,
        pre_outer,
        query_weight,
        history_kv,
        history_bias,
        expert_weight,
        gate_weight,
        tower_inner,
        tower_outer,
    )
    return score, jnp.transpose(rank, (1, 0, 2))


def solution(mesh):
    return jax.shard_map(
        on_device,
        mesh=mesh,
        in_specs=(
            P("groups", ("wide", "narrow"), None),
            P(),
            P(),
            P(),
            P("groups", None),
            P("groups", None),
            P("groups"),
            P(("groups", "wide"), None, None, "narrow"),
            P(("groups", "wide"), "narrow", None),
            P(("groups", "wide")),
            P(),
            P(),
            P("narrow", None, None),
            P(),
            P(),
            P("narrow", None, None),
            P("narrow", None),
        ),
        out_specs=(P("groups", ("wide", "narrow")), P(None, "groups", ("wide", "narrow"))),
        check_vma=False,
    )
```

time: 110 us -> 36.9 us (0.34)
  Pallas kernels: 0 us -> 30.5 us
  matrix products: 18.6 us -> 0 us
  between operations: 17.1 us -> 1.3 us
  waiting for transfers between devices: 14.7 us -> 0 us
  other arithmetic: 15.1 us -> 0.63 us
  local copies, waits for them, and re-layouts: 17.9 us -> 4.22 us
  starting transfers between devices: 13.1 us -> 0 us
  blocking collectives: 12.4 us -> 0 us
    pallas_call x0 -> x1, Pallas kernels: none -> 30.5 us  [on_device(): pl.pallas_call(functools.partial(cascade, wide, narrow, block), out_shape...]
    dot_general x9 -> x0, matrix products: 14.7 us -> none  [the longest x1 3.14 us: on_device(): jnp.einsum('kte,keh->kth', gate_probs, lax.all_gather(expert_out, 'narrow...]
    all_to_all x2 -> x0, starting transfers between devices: 13.1 us -> none  [the longest x1 7.28 us: on_device(): lax.all_to_all(sending, 'wide', split_axis=0, concat_axis=1, tiled=True)]
    gather x10 -> x0, local copies, waits for them, and re-layouts: 10.2 us -> none  [the longest x2 3.02 us: on_device(): jnp.take_along_axis(task_logit, source_rows[:, :, None], axis=1)]
    all_gather x1 -> x0, waiting for transfers between devices: 8.12 us -> none  [on_device(): lax.all_gather(expert_out, 'narrow', axis=1, tiled=True)]
    all_to_all x2 -> x0, blocking collectives: 7.88 us -> none  [the longest x1 4.15 us: on_device(): lax.all_to_all(lax.all_to_all(sending, 'wide', split_axis=0, concat_axis=...]
    all_to_all x2 -> x0, waiting for transfers between devices: 6.57 us -> none  [the longest x1 6.57 us: on_device(): lax.all_to_all(returning, 'wide', split_axis=2, concat_axis=0, tiled=True)]
    and x2 -> x0, other arithmetic: 5.69 us -> none  [the longest x1 5.6 us: on_device(): jnp.take_along_axis(arrived.reshape(group_size, shards * capacity, -1), f...]
  transfers between devices with their start and end apart: 3 -> 0, of which waited for: 2 -> 0; matrix products, arithmetic and copies ran while one was open for 16% -> 0% of each run, Pallas kernels for 0% -> 0%
where the time goes in v1:
time: 36.9 us; the launch traced here: 36.6 us
  Pallas kernels  30.5 us (83%)
  local copies, waits for them, and re-layouts  4.22 us (11%)
  between operations  1.3 us (4%)
  other arithmetic  0.63 us (2%)
    pallas_call x1, Pallas kernels, on_device(): pl.pallas_call(functools.partial(cascade, wide, narrow, block), out_shape...  30.5 us
    unnamed x7, local copies, waits for them, and re-layouts  4.22 us

profile of v1, /device:TPU:0, one launch (start us, length us, event | category | flops | bytes accessed | tf_op | source)
XLA Modules:
  0.0 36.6 jit_solution(8294504523275760284)
XLA Ops:
  1.3 0.0 copy-start.1
  1.3 0.6 %copy-done.1 = s32[8]{0:T(128)S(1)} copy-done((s32[8]{0:T(128)S(1)}, s32[8]{0:T(128)}, u32[]{:S(2)}) %copy-start.1) | copy-done | bytes 56
  1.9 0.6 %select_reduce_fusion.slot_of = s32[8]{0:T(128)} fusion(s32[8]{0:T(128)S(1)} %copy-done.1), kind=kLoop, calls=%fused_computation | loop fusion | flops 184 | bytes 64 | tf_op jit(solution)/shard_map/reduce_sum | solution.py:433
  2.6 1.6 %copy.21.gate_hbm = bf16[512,64]{1,0:T(8,128)(2,1)} copy(bf16[512,64]{0,1:T(8,128)(2,1)} %param.30) | data formatting | bytes 131072 | tf_op args[13]
  4.2 30.5 %shard_map.176 = (f32[8,128]{1,0:T(8,128)}, f32[8,8,128]{2,1,0:T(8,128)}) custom-call(s32[8]{0:T(128)} %slot_request.1, s32[8]{0:T(128)} %select_reduce_fusion.slot_of, s32[1]{0:T(128)S(6)} %copy.24.length, s32[8,512]{1,0:T(8,128)} %kept.1, bf16[8,512]{1,0:T(8,128)(2,1)} %user.1, f32[1,512]{1,0:T(1,128)} %bitcast.4, f32[1,512]{1,0:T(1,128)} %bitcast.5, ...), custom_call_target="tpu_custom_call" | custom-call | tf_op jit(solution)/shard_map/pallas_call | solution.py:444
  34.6 0.0 copy-start
  34.6 1.4 %copy.22 = f32[8,8,128]{2,1,0:T(8,128)} copy(f32[8,8,128]{2,0,1:T(8,128)} %bitcast.3) | data formatting | bytes 65536
  36.0 0.0 copy-done
  36.0 0.6 %copy.25 = f32[8,128]{1,0:T(8,128)} copy(f32[8,128]{1,0:T(8,128)S(1)} %copy-done) | data formatting | bytes 8192
Async XLA Ops:
  1.3 0.7 %copy-start.1 = (s32[8]{0:T(128)S(1)}, s32[8]{0:T(128)}, u32[]{:S(2)}) copy-start(s32[8]{0:T(128)} %slot_request.1) | copy-start | bytes 100
  34.6 1.4 %copy-start = (f32[8,128]{1,0:T(8,128)S(1)}, f32[8,128]{1,0:T(8,128)}, u32[]{:S(2)}) copy-start(f32[8,128]{1,0:T(8,128)} %get-tuple-element.12) | copy-start | bytes 12292

commit v2 on v1

--- a/solution.py
+++ b/solution.py
@@ -39,7 +39,6 @@
     narrow,
     block,
     slot_request,
-    slot_of,
     length,
     kept,
     user,
@@ -297,7 +296,7 @@
         u * lax.rsqrt(jnp.mean(u * u, axis=1, keepdims=True) + 1e-06) * norm_gain[...]
     ).astype(BF16)
 
-    logits = dot(gate[...], normed, ((0,), (1,)))
+    logits = dot(gate[...], normed, ((1,), (1,)))
     diagonal = iota((experts, experts), 0) == iota((experts, experts), 1)
     probs = []
     for t in range(tasks):
@@ -377,10 +376,18 @@
     loop(shards - 1, back_in)
 
     def deliver(r):
-        total = returned[slot_of[r] * narrow]
+        if requests <= 16:
+            slot = 0
+            for g in range(requests):
+                slot = jnp.where(slot_request[g] == r, g, slot)
+        else:
+            slot = lax.fori_loop(
+                0, requests, lambda g, a: jnp.where(slot_request[g] == r, g, a), 0
+            )
+        total = returned[slot * narrow]
         for p in range(1, narrow):
-            total = total + returned[slot_of[r] * narrow + p]
-        rank_out[r] = total[:, :shard_len]
+            total = total + returned[slot * narrow + p]
+        rank_out[:, r, :] = total[:, :shard_len]
 
     loop(requests, deliver)
 
@@ -429,8 +436,6 @@
     tasks, experts = gate_bias.shape
     hidden = expert_weight.shape[2]
     lanes = max(shard_len, 128)
-    ids = jnp.arange(requests, dtype=jnp.int32)
-    slot_of = jnp.sum(jnp.where(slot_request[None, :] == ids[:, None], ids[None, :], 0), axis=1)
     smem = pl.BlockSpec(memory_space=pltpu.SMEM)
     vmem = pl.BlockSpec(memory_space=pltpu.VMEM)
     hbm = pl.BlockSpec(memory_space=pl.ANY)
@@ -445,9 +450,9 @@
         functools.partial(cascade, wide, narrow, block),
         out_shape=(
             jax.ShapeDtypeStruct((requests, shard_len), F32),
-            jax.ShapeDtypeStruct((requests, tasks, shard_len), F32),
+            jax.ShapeDtypeStruct((tasks, requests, shard_len), F32),
         ),
-        in_specs=[smem] * 3 + [vmem] * 5 + [hbm] * 10,
+        in_specs=[smem] * 2 + [vmem] * 5 + [hbm] * 10,
         out_specs=(vmem, vmem),
         scratch_shapes=[
             whole(candidates),
@@ -457,7 +462,7 @@
             pltpu.VMEM((narrow, *history_kv.shape[1:]), BF16),
             pltpu.VMEM((narrow, *history_bias.shape[1:]), F32),
             both(expert_weight),
-            whole(gate_weight),
+            pltpu.VMEM(gate_weight.shape[::-1], BF16),
             both(tower_inner),
             both(tower_outer),
             pltpu.VMEM((wide, narrow, block, width), BF16),
@@ -480,7 +485,6 @@
         ),
     )(
         slot_request,
-        slot_of,
         history_length,
         kept_index,
         user_vector,
@@ -494,11 +498,11 @@
         history_kv,
         history_bias,
         expert_weight,
-        gate_weight,
+        gate_weight.T,
         tower_inner,
         tower_outer,
     )
-    return score, jnp.transpose(rank, (1, 0, 2))
+    return score, rank
 
 
 def solution(mesh):

time: 36.9 us -> 34.7 us (0.940)
  local copies, waits for them, and re-layouts: 4.22 us -> 2.65 us
  other arithmetic: 0.63 us -> 0 us
    unnamed x7 -> x2, local copies, waits for them, and re-layouts: 4.22 us -> 2.65 us
    reduce_sum x1 -> x0, other arithmetic: 0.63 us -> none  [on_device(): jnp.sum(jnp.where(slot_request[None, :] == ids[:, None], ids[None, :], 0)...]
where the time goes in v2:
time: 34.7 us; the launch traced here: 34.4 us
  Pallas kernels  30.5 us (88%)
  local copies, waits for them, and re-layouts  2.65 us (8%)
  between operations  1.29 us (4%)
    pallas_call x1, Pallas kernels, on_device(): pl.pallas_call(functools.partial(cascade, wide, narrow, block), out_shape...  30.5 us
    unnamed x2, local copies, waits for them, and re-layouts  2.65 us

profile of v2, /device:TPU:0, one launch (start us, length us, event | category | flops | bytes accessed | tf_op | source)
XLA Modules:
  0.0 34.4 jit_solution(273973910006629127)
XLA Ops:
  1.3 30.5 %shard_map.176 = (f32[8,128]{1,0:T(8,128)}, f32[8,8,128]{2,1,0:T(8,128)}) custom-call(s32[8]{0:T(128)} %slot_request.1, s32[1]{0:T(128)S(6)} %copy.21.length, s32[8,512]{1,0:T(8,128)} %kept.1, bf16[8,512]{1,0:T(8,128)(2,1)} %user.1, f32[1,512]{1,0:T(1,128)} %bitcast.4, f32[1,512]{1,0:T(1,128)} %bitcast.5, f32[8,8]{1,0:T(8,128)} %gate_bias.1, ...), custom_call_target="tpu_custom_call" | custom-call | tf_op jit(solution)/shard_map/pallas_call | solution.py:449
  31.8 1.3 %copy.22 = f32[8,128]{1,0:T(8,128)} copy(f32[8,128]{1,0:T(8,128)} %get-tuple-element.4) | data formatting | bytes 8192
  33.0 1.4 %copy.23 = f32[8,8,128]{2,1,0:T(8,128)} copy(f32[8,8,128]{2,1,0:T(8,128)} %get-tuple-element.5) | data formatting | bytes 65536
